TPU v7x, 32 devices: a whole 2x2x4 slice. The times are simulated.
32 devices in a mesh: tile: 2 (over y), pts: 4 (over z), head: 4 (over x, core).
Axes of the slice: x: 2, y: 2, z: 4, core: 2. Of those that a mesh axis runs over, the one named last changes fastest.
Arguments:
- z_feat: bfloat16 [24544, 512], P(('tile', 'pts')), parts along dimension 0, may hold values from -12 to 12
- shard_count: int32 [8], P(('tile', 'pts')), parts along dimension 0, may hold values from 1028 to 3068, as said below
- hilbert_rank: int32 [24544], P(('tile', 'pts')), parts along dimension 0, may hold values from 0 to 8191, as said below
- z_slot: int32 [16384], P(('tile', 'pts')), parts along dimension 0, may hold values from 0 to 12271, as said below
- ln1_gain: float32 [512], replicated, may hold values from 0.25 to 1.75
- ln1_bias: float32 [512], replicated, may hold values from -1.5 to 1.5
- w_qkv: bfloat16 [3, 512, 512], P(None, None, 'head'), may hold values from -16 to 16
- w_out: bfloat16 [512, 512], P(None, 'head'), may hold values from -0.25 to 0.25
- b_out: float32 [512], P('head'), may hold values from -2.5 to 2.5
- ln2_gain: float32 [512], replicated, may hold values from 0.25 to 1.75
- ln2_bias: float32 [512], replicated, may hold values from -1.5 to 1.5
- w_up: bfloat16 [512, 2048], P(None, 'head'), may hold values from -0.25 to 0.25
- b_up: float32 [2048], P('head'), may hold values from -2.5 to 2.5
- w_down: bfloat16 [2048, 512], P('head'), may hold values from -0.125 to 0.125
- b_down: float32 [512], P('head'), may hold values from -2.5 to 2.5
Outputs:
- z_out: bfloat16 [24544, 512], P(('tile', 'pts'), 'head'), parts along dimension 0
There are 2 independent parts, one for each index of `tile`. A program takes and returns all parts, laid end to end along the dimension named above; an argument that names none is the same for every part. Nothing has to cross between parts.
Inputs may be any that keep to these rules, and one draw needn't show every extreme that they name: `shard_count`: the number of points of z-order shard s, held in the first that many of its 3068 slots; the counts sum to 8192; some shard holds 3068 points. `hilbert_rank`: on occupied slots, a one to one map onto the 8192 Hilbert positions; empty slots hold 0; of the points of one z-order shard at most 1022 lie among the 2048 Hilbert positions of one index of pts, and some shard and index reach 1022. `z_slot`: the inverse of hilbert_rank: for Hilbert position h, the occupied slot whose hilbert_rank is h.
All inputs are finite; a program needn't handle non-finite values.
Results may differ from a plain program's by a relative error of at most 0.013.
Values may be sent and summed in bfloat16 or wider, within the bound.
No kernel may reach another device: no remote copies, remote signals or barrier semaphores. Data moves between devices by JAX's collectives and lax.ppermute only.
A program may use at most 64 MiB of HBM per device.

v0:
```python
import jax
import jax.numpy as jnp
from jax import lax
from jax.sharding import PartitionSpec as P

PATCH = 1024
HEAD_DIM = 16


def layer_norm(widened, norm_gain, norm_bias):
    width = widened.shape[1]
    row_mean = jnp.sum(widened, axis=1, keepdims=True) / width
    row_square = jnp.sum(widened * widened, axis=1, keepdims=True) / width
    row_var = row_square - row_mean * row_mean
    return (widened - row_mean) * lax.rsqrt(row_var + 1e-05) * norm_gain + norm_bias


def slot_layout(hilbert_rank, count_here, rows_here, shards, slot_cap):
    slot_ids = jnp.arange(hilbert_rank.shape[0], dtype=jnp.int32)
    occupied = slot_ids < count_here
    target = hilbert_rank // rows_here
    onehot = (
        (target[:, None] == jnp.arange(shards, dtype=jnp.int32)[None, :]) & occupied[:, None]
    ).astype(jnp.int32)
    earlier = jnp.cumsum(onehot, axis=0) - onehot
    bucket = jnp.sum(earlier * onehot, axis=1)
    send_at = jnp.where(occupied, target * slot_cap + bucket, shards * slot_cap)
    return (occupied, send_at)


def arrival_layout(z_slot, zone_rows, shards, slot_cap):
    rows_here = z_slot.shape[0]
    source = z_slot // zone_rows
    order = jnp.argsort(z_slot)
    sorted_rank = (
        jnp.zeros((rows_here,), jnp.int32).at[order].set(jnp.arange(rows_here, dtype=jnp.int32))
    )
    shard_ids = jnp.arange(shards, dtype=jnp.int32)
    below = jnp.sum((z_slot[:, None] < (shard_ids * zone_rows)[None, :]).astype(jnp.int32), axis=0)
    first = jnp.sum(jnp.where(source[:, None] == shard_ids[None, :], below[None, :], 0), axis=1)
    return source * slot_cap + sorted_rank - first


def attend_blocks(queries, key_rows, value_rows, heads_here):
    rows_here = queries.shape[0]
    block_rows = min(512, PATCH)
    per_patch = PATCH // block_rows
    query_blocks = queries.reshape(rows_here // block_rows, block_rows, heads_here, HEAD_DIM)
    key_patches = key_rows.reshape(rows_here // PATCH, PATCH, heads_here, HEAD_DIM)
    value_patches = value_rows.reshape(rows_here // PATCH, PATCH, heads_here, HEAD_DIM)
    score_scale = HEAD_DIM ** (-0.5)

    def one_block(carried):
        block_query, block_idx = carried
        patch_idx = block_idx // per_patch
        patch_keys = lax.dynamic_index_in_dim(key_patches, patch_idx, 0, keepdims=False)
        patch_values = lax.dynamic_index_in_dim(value_patches, patch_idx, 0, keepdims=False)
        scores = (
            jnp.einsum("qhd,khd->hqk", block_query, patch_keys, preferred_element_type=jnp.float32)
            * score_scale
        )
        raised = jnp.exp(scores - jnp.max(scores, axis=2, keepdims=True))
        weights_bf = (raised / jnp.sum(raised, axis=2, keepdims=True)).astype(jnp.bfloat16)
        return jnp.einsum(
            "hqk,khd->qhd", weights_bf, patch_values, preferred_element_type=jnp.float32
        ).astype(jnp.bfloat16)

    mixed = lax.map(one_block, (query_blocks, jnp.arange(rows_here // block_rows, dtype=jnp.int32)))
    return mixed.reshape(rows_here, heads_here * HEAD_DIM)


def body(
    z_feat,
    shard_count,
    hilbert_rank,
    z_slot,
    ln1_gain,
    ln1_bias,
    w_qkv,
    w_out,
    b_out,
    ln2_gain,
    ln2_bias,
    w_up,
    b_up,
    w_down,
    b_down,
):
    shards = lax.axis_size("pts")
    rows_here = z_slot.shape[0]
    zone_rows = z_feat.shape[0]
    skew_step = rows_here // (2 * shards * (shards - 1))
    slot_cap = rows_here // shards + 2 * skew_step * (shards - 1)
    col_width = w_out.shape[1]
    col_start = lax.axis_index("head") * col_width
    occupied, send_at = slot_layout(hilbert_rank, shard_count[0], rows_here, shards, slot_cap)
    arrive_at = arrival_layout(z_slot, zone_rows, shards, slot_cap)

    def pack_rows(rows, where_to, slots_total):
        width = rows.shape[1]
        filled = jnp.zeros((slots_total, width), rows.dtype).at[where_to].set(rows, mode="drop")
        return filled.reshape(shards, slot_cap, width)

    own_columns = lax.dynamic_slice_in_dim(z_feat, col_start, col_width, 1)
    arrived = lax.all_to_all(
        pack_rows(own_columns, send_at, shards * slot_cap),
        "pts",
        split_axis=0,
        concat_axis=0,
        tiled=True,
    )
    feat_cols = arrived.reshape(shards * slot_cap, arrived.shape[2])[arrive_at]
    features = lax.all_gather(feat_cols, "head", axis=1, tiled=True)
    normed = layer_norm(features.astype(jnp.float32), ln1_gain, ln1_bias).astype(jnp.bfloat16)
    projected = jnp.einsum("pc,tcd->tpd", normed, w_qkv, preferred_element_type=jnp.float32).astype(
        jnp.bfloat16
    )
    heads_here = col_width // HEAD_DIM
    attended = attend_blocks(projected[0], projected[1], projected[2], heads_here)
    weight_rows = w_out
    projected_out = jnp.dot(
        lax.all_gather(attended, "head", axis=1, tiled=True),
        weight_rows,
        preferred_element_type=jnp.float32,
    )
    residual = (feat_cols.astype(jnp.float32) + projected_out + b_out).astype(jnp.bfloat16)
    full_width = w_up.shape[0]
    widened = residual.astype(jnp.float32)
    row_sum, row_squares = lax.psum(
        (jnp.sum(widened, axis=1), jnp.sum(widened * widened, axis=1)), "head"
    )
    row_mean = row_sum / full_width
    row_var = row_squares / full_width - row_mean * row_mean
    gain_cols = lax.dynamic_slice_in_dim(ln2_gain, col_start, col_width, 0)
    bias_cols = lax.dynamic_slice_in_dim(ln2_bias, col_start, col_width, 0)
    normed_cols = (
        (widened - row_mean[:, None]) * lax.rsqrt(row_var + 1e-05)[:, None] * gain_cols + bias_cols
    ).astype(jnp.bfloat16)
    weight_rows = w_up
    pre_gelu = jnp.dot(
        lax.all_gather(normed_cols, "head", axis=1, tiled=True),
        weight_rows,
        preferred_element_type=jnp.float32,
    )
    hidden = jax.nn.gelu(pre_gelu + b_up, approximate=False).astype(jnp.bfloat16)
    partial_down = jnp.dot(hidden, w_down, preferred_element_type=jnp.float32)
    down_cols = lax.psum_scatter(
        partial_down.astype(jnp.bfloat16), "head", scatter_dimension=1, tiled=True
    ).astype(jnp.float32)
    block_out = (residual.astype(jnp.float32) + down_cols + b_down).astype(jnp.bfloat16)
    outgoing = pack_rows(block_out, arrive_at, shards * slot_cap)
    returned = lax.all_to_all(outgoing, "pts", split_axis=0, concat_axis=0, tiled=True).reshape(
        shards * slot_cap, col_width
    )
    picked = returned[jnp.minimum(send_at, shards * slot_cap - 1)]
    return jnp.where(occupied[:, None], picked, jnp.zeros_like(picked))


def solution(mesh):
    placed = (
        P(("tile", "pts"), None),
        P(("tile", "pts")),
        P(("tile", "pts")),
        P(("tile", "pts")),
        P(),
        P(),
        P(None, None, "head"),
        P(None, "head"),
        P("head"),
        P(),
        P(),
        P(None, "head"),
        P("head"),
        P("head", None),
        P("head"),
    )
    return jax.shard_map(
        body, mesh=mesh, in_specs=placed, out_specs=P(("tile", "pts"), "head"), check_vma=False
    )
```

profile of v0, /device:TPU:0, one launch (start us, length us, event | category | flops | bytes accessed | tf_op | source)
XLA Modules:
  0.0 362.1 jit_solution(17592234452725337201)
XLA Ops:
  11.4 12.6 %scatter_custom_fusion.1 = bf16[4088,128]{1,0:T(8,128)(2,1)} fusion(s32[3068]{0:T(1024)S(1)} %get-tuple-element.128, bf16[3068,512]{1,0:T(8,128)(2,1)S(1)} %copy-done, s32[]{:T(128)} %constant.145.clone.1, s32[]{:T(128)S(6)} %select_n.63, bf16[]{:T(256)} %constant.80.clone.1), kind=kCustom, calls=%fused_computation.75 | custom fusion | bytes 1832970 | tf_op jit(solution)/shard_map/scatter | solution.py:101
  23.9 2.5 reshape.69
  26.5 6.3 %all-to-all-start = ((bf16[4,1022,128]{2,1,0:T(8,128)(2,1)}), bf16[4,1022,128]{2,1,0:T(8,128)(2,1)}, u32[]{:S(2)}, u32[]{:S(2)}) async-start(bf16[4,1022,128]{2,1,0:T(8,128)(2,1)} %reshape.69), calls=%async_computation | async-start | bytes 2097152 | tf_op jit(solution)/shard_map/all_to_all | solution.py:105
  32.8 5.0 %sort.17 = (s32[2048]{0:T(1024)}, s32[2048]{0:T(1024)S(1)}) sort(s32[2048]{0:T(1024)S(1)} %copy-done.1, s32[2048]{0:T(1024)S(1)} %iota.27), dimensions={0}, to_apply=%region_0.1 | sort | flops 22528 | bytes 32768 | tf_op jit(solution)/shard_map/jit(argsort)/sort | solution.py:34
  37.9 8.0 %scatter_custom_fusion = s32[2048]{0:T(1024)S(1)} fusion(s32[2048]{0:T(1024)S(1)} %compare_select_fusion.3, s32[2048]{0:T(1024)S(1)} %iota.28, s32[]{:T(128)} %constant.145.clone.1), kind=kCustom, calls=%fused_computation.119 | custom fusion | bytes 8196 | tf_op jit(solution)/shard_map/scatter | solution.py:36
  46.9 11.8 %all-to-all-done = bf16[4,1022,128]{2,1,0:T(8,128)(2,1)} async-done(((bf16[4,1022,128]{2,1,0:T(8,128)(2,1)}), bf16[4,1022,128]{2,1,0:T(8,128)(2,1)}, u32[]{:S(2)}, u32[]{:S(2)}) %all-to-all-start) | async-done | bytes 1046560 | tf_op jit(solution)/shard_map/all_to_all | solution.py:105
  58.7 2.5 reshape.70
  61.2 9.1 %gather_fusion = bf16[2048,128]{1,0:T(8,128)(2,1)} fusion(bf16[4088,128]{1,0:T(8,128)(2,1)} %reshape.70, s32[2048]{0:T(1024)S(1)} %get-tuple-element.122), kind=kCustom, calls=%fused_computation | custom fusion | bytes 1056768 | tf_op jit(solution)/shard_map/gather | solution.py:112
  70.3 22.0 %all-gather.9.cloned.1.call-done = bf16[2048,512]{1,0:T(8,128)(2,1)} async-done(((bf16[2048,128]{1,0:T(8,128)(2,1)}), bf16[2048,512]{1,0:T(8,128)(2,1)}) %all-gather.9.cloned.1.call-update) | async-done | bytes 2097168 | tf_op jit(solution)/shard_map/all_gather | solution.py:113
  94.6 3.0 fusion.83
  117.6 65.4 %while.12 = (s32[]{:T(128)}, bf16[4,512,8,16]{1,3,2,0:T(8,128)(2,1)}, s32[4]{0:T(128)S(1)}, bf16[2,1024,8,16]{1,3,2,0:T(8,128)(2,1)}, bf16[4,512,8,16]{1,3,2,0:T...) while((s32[]{:T(128)}, ...), condition=%wide.region_13.14_spmd, body=%wide.region_10.13_spmd.sunk | while | flops 432084992 | bytes 1214777 | solution.py:68
  120.7 5.8 %fusion.168 = f32[8,512]{1,0:T(8,128)S(1)} fusion(bf16[2,1024,8,16]{1,3,2,0:T(8,128)(2,1)} %get-tuple-element.196, s32[]{:T(128)S(6)} %select_n.90, bf16[4,512,8,16]{1,3,2,0:T(8,128)(2,1)} %get-tuple-element.195, s32[]{:T(128)S(6)} %copy.52), kind=kOutput, calls=%fused_computation.153.clone.1 | convolution fusion | flops 146801664 | bytes 409608 | tf_op jit(solution)/shard_map/while/body/eval_jaxpr/sub | solution.py:62
  126.5 7.5 %fusion.169 = bf16[4,512,8,16]{1,3,2,0:T(8,128)(2,1)} fusion(bf16[4,512,8,16]{1,3,2,0:T(8,128)(2,1)} %get-tuple-element.182, s32[]{:T(128)S(6)} %copy.52, f32[8,512]{1,0:T(8,128)S(1)} %fusion.168, bf16[2,1024,8,16]{1,3,2,0:T(8,128)(2,1)} %get-tuple-element.194, s32[]{:T(128)S(6)} %select_n.90, bf16[2,1024,8,16]{1,3,2,0:T(8,128)(2,1)} %get-tuple-element.196, ...), kind=kOutput, calls=%fused_computation.15.clone.1 | convolution fusion | flops 285283328 | bytes 804864 | tf_op jit(solution)/shard_map/while/body/eval_jaxpr/hqk,khd->qhd/dot_general | solution.py:64
  137.0 5.8 %fusion.168 = f32[8,512]{1,0:T(8,128)S(1)} fusion(bf16[2,1024,8,16]{1,3,2,0:T(8,128)(2,1)} %get-tuple-element.196, s32[]{:T(128)S(6)} %select_n.90, bf16[4,512,8,16]{1,3,2,0:T(8,128)(2,1)} %get-tuple-element.195, s32[]{:T(128)S(6)} %copy.52), kind=kOutput, calls=%fused_computation.153.clone.1 | convolution fusion | flops 146801664 | bytes 409608 | tf_op jit(solution)/shard_map/while/body/eval_jaxpr/sub | solution.py:62
  142.9 7.5 %fusion.169 = bf16[4,512,8,16]{1,3,2,0:T(8,128)(2,1)} fusion(bf16[4,512,8,16]{1,3,2,0:T(8,128)(2,1)} %get-tuple-element.182, s32[]{:T(128)S(6)} %copy.52, f32[8,512]{1,0:T(8,128)S(1)} %fusion.168, bf16[2,1024,8,16]{1,3,2,0:T(8,128)(2,1)} %get-tuple-element.194, s32[]{:T(128)S(6)} %select_n.90, bf16[2,1024,8,16]{1,3,2,0:T(8,128)(2,1)} %get-tuple-element.196, ...), kind=kOutput, calls=%fused_computation.15.clone.1 | convolution fusion | flops 285283328 | bytes 804864 | tf_op jit(solution)/shard_map/while/body/eval_jaxpr/hqk,khd->qhd/dot_general | solution.py:64
  153.4 5.8 %fusion.168 = f32[8,512]{1,0:T(8,128)S(1)} fusion(bf16[2,1024,8,16]{1,3,2,0:T(8,128)(2,1)} %get-tuple-element.196, s32[]{:T(128)S(6)} %select_n.90, bf16[4,512,8,16]{1,3,2,0:T(8,128)(2,1)} %get-tuple-element.195, s32[]{:T(128)S(6)} %copy.52), kind=kOutput, calls=%fused_computation.153.clone.1 | convolution fusion | flops 146801664 | bytes 409608 | tf_op jit(solution)/shard_map/while/body/eval_jaxpr/sub | solution.py:62
  159.2 7.5 %fusion.169 = bf16[4,512,8,16]{1,3,2,0:T(8,128)(2,1)} fusion(bf16[4,512,8,16]{1,3,2,0:T(8,128)(2,1)} %get-tuple-element.182, s32[]{:T(128)S(6)} %copy.52, f32[8,512]{1,0:T(8,128)S(1)} %fusion.168, bf16[2,1024,8,16]{1,3,2,0:T(8,128)(2,1)} %get-tuple-element.194, s32[]{:T(128)S(6)} %select_n.90, bf16[2,1024,8,16]{1,3,2,0:T(8,128)(2,1)} %get-tuple-element.196, ...), kind=kOutput, calls=%fused_computation.15.clone.1 | convolution fusion | flops 285283328 | bytes 804864 | tf_op jit(solution)/shard_map/while/body/eval_jaxpr/hqk,khd->qhd/dot_general | solution.py:64
  169.8 5.8 %fusion.168 = f32[8,512]{1,0:T(8,128)S(1)} fusion(bf16[2,1024,8,16]{1,3,2,0:T(8,128)(2,1)} %get-tuple-element.196, s32[]{:T(128)S(6)} %select_n.90, bf16[4,512,8,16]{1,3,2,0:T(8,128)(2,1)} %get-tuple-element.195, s32[]{:T(128)S(6)} %copy.52), kind=kOutput, calls=%fused_computation.153.clone.1 | convolution fusion | flops 146801664 | bytes 409608 | tf_op jit(solution)/shard_map/while/body/eval_jaxpr/sub | solution.py:62
  175.6 7.5 %fusion.169 = bf16[4,512,8,16]{1,3,2,0:T(8,128)(2,1)} fusion(bf16[4,512,8,16]{1,3,2,0:T(8,128)(2,1)} %get-tuple-element.182, s32[]{:T(128)S(6)} %copy.52, f32[8,512]{1,0:T(8,128)S(1)} %fusion.168, bf16[2,1024,8,16]{1,3,2,0:T(8,128)(2,1)} %get-tuple-element.194, s32[]{:T(128)S(6)} %select_n.90, bf16[2,1024,8,16]{1,3,2,0:T(8,128)(2,1)} %get-tuple-element.196, ...), kind=kOutput, calls=%fused_computation.15.clone.1 | convolution fusion | flops 285283328 | bytes 804864 | tf_op jit(solution)/shard_map/while/body/eval_jaxpr/hqk,khd->qhd/dot_general | solution.py:64
  189.1 19.1 %all-gather.5.cloned.1.call-done = bf16[2048,512]{0,1:T(8,128)(2,1)} async-done(((bf16[2048,128]{0,1:T(8,128)(2,1)}), bf16[2048,512]{0,1:T(8,128)(2,1)}) %all-gather.5.cloned.1.call-update) | async-done | bytes 2097168 | tf_op jit(solution)/shard_map/all_gather | solution.py:122
  208.2 3.2 fusion.137
  211.4 10.2 %all-reduce.1 = (f32[2048]{0:T(1024)S(1)}, f32[2048]{0:T(1024)S(1)}) all-reduce(f32[2048]{0:T(1024)S(1)} %get-tuple-element.107, f32[2048]{0:T(1024)S(1)} %get-tuple-element.106), channel_id=1, replica_groups=mesh['tile'=2,'pts'=4,'head'=4] {'head'}, use_global_device_ids=true, to_apply=%region_17.18 | all-reduce | flops 4096 | bytes 32768 | tf_op jit(solution)/shard_map/psum | solution.py:129
  224.0 23.7 %all-gather.7.cloned.1.call-done = bf16[2048,512]{0,1:T(8,128)(2,1)} async-done(((bf16[2048,128]{0,1:T(8,128)(2,1)}), bf16[2048,512]{0,1:T(8,128)(2,1)}) %all-gather.7.cloned.1.call-update) | async-done | bytes 2097168 | tf_op jit(solution)/shard_map/all_gather | solution.py:141
  247.8 13.8 %convolution_convert_fusion = bf16[2048,512]{0,1:T(8,128)(2,1)} fusion(bf16[512,512]{1,0:T(8,128)(2,1)} %param.30, bf16[2048,512]{0,1:T(8,128)(2,1)} %all-gather.7.cloned.1.call-done, bf16[512,512]{1,0:T(8,128)(2,1)} %param.28, f32[512]{0:T(512)S(1)} %copy-done.10), kind=kOutput, calls=%fused_computation.60 | convolution fusion | flops 2217738240 | bytes 5244928 | tf_op jit(solution)/shard_map/dot_general | solution.py:146
  261.6 31.3 %reduce-scatter.2.cloned.1.call-done = bf16[2048,128]{0,1:T(8,128)(2,1)} async-done(((bf16[2048,512]{0,1:T(8,128)(2,1)}), bf16[2048,128]{0,1:T(8,128)(2,1)}) %reduce-scatter.2.cloned.1.call-update) | async-done | bytes 524304 | tf_op jit(solution)/shard_map/reduce_scatter | solution.py:147
  297.3 7.2 %scatter_custom_fusion.2 = bf16[4088,128]{1,0:T(8,128)(2,1)} fusion(s32[2048]{0:T(1024)} %get-tuple-element.123, bf16[2048,128]{1,0:T(8,128)(2,1)} %copy.40, bf16[]{:T(256)} %constant.80.clone.1), kind=kCustom, calls=%fused_computation.78 | custom fusion | bytes 1047040 | tf_op jit(solution)/shard_map/scatter | solution.py:101
  304.5 2.5 reshape.72
  307.0 4.6 %all-to-all-start.1 = ((bf16[4,1022,128]{2,1,0:T(8,128)(2,1)}), bf16[4,1022,128]{2,1,0:T(8,128)(2,1)}, u32[]{:S(2)}, u32[]{:S(2)}) async-start(bf16[4,1022,128]{2,1,0:T(8,128)(2,1)} %reshape.72), calls=%async_computation.2 | async-start | bytes 2097152 | tf_op jit(solution)/shard_map/all_to_all | solution.py:152
  311.7 25.6 %all-to-all-done.1 = bf16[4,1022,128]{2,1,0:T(8,128)(2,1)} async-done(((bf16[4,1022,128]{2,1,0:T(8,128)(2,1)}), bf16[4,1022,128]{2,1,0:T(8,128)(2,1)}, u32[]{:S(2)}, u32[]{:S(2)}) %all-to-all-start.1) | async-done | bytes 1046560 | tf_op jit(solution)/shard_map/all_to_all | solution.py:152
  337.3 2.5 reshape.73
  339.8 12.4 %gather_fusion.1 = bf16[3068,128]{1,0:T(8,128)(2,1)} fusion(bf16[4088,128]{1,0:T(8,128)(2,1)} %reshape.73, s32[3072]{0:T(1024)S(1)} %pad_clamp_fusion), kind=kCustom, calls=%fused_computation.1 | custom fusion | bytes 1583088 | tf_op jit(solution)/shard_map/gather | solution.py:155
  352.3 3.3 broadcast_select_fusion
  (80 shorter events, 42.4 us)
Async XLA Ops:
  6.5 4.9 %copy-start = (bf16[3068,512]{1,0:T(8,128)(2,1)S(1)}, bf16[3068,512]{1,0:T(8,128)(2,1)}, u32[]{:S(2)}) copy-start(bf16[3068,512]{1,0:T(8,128)(2,1)} %param.17) | copy-start | bytes 9424900
  7.4 19.1 %copy-start.3 = (pred[3068]{0:T(1024)(128)(4,1)}, pred[3068]{0:T(1024)(128)(4,1)S(1)}, u32[]{:S(2)}) copy-start(pred[3068]{0:T(1024)(128)(4,1)S(1)} %iota_compare_fusion.3) | copy-start | bytes 9208
  10.0 22.9 %copy-start.1 = (s32[2048]{0:T(1024)S(1)}, s32[2048]{0:T(1024)}, u32[]{:S(2)}) copy-start(s32[2048]{0:T(1024)} %param.20) | copy-start | bytes 24580
  26.5 32.2 %all-to-all-start = ((bf16[4,1022,128]{2,1,0:T(8,128)(2,1)}), bf16[4,1022,128]{2,1,0:T(8,128)(2,1)}, u32[]{:S(2)}, u32[]{:S(2)}) async-start(bf16[4,1022,128]{2,1,0:T(8,128)(2,1)} %reshape.69), calls=%async_computation | async-start | bytes 2097152 | tf_op jit(solution)/shard_map/all_to_all | solution.py:105
  32.8 59.5 %all-gather.9.cloned.1.call-start = ((), (), s32[]{:S(2)}) async-start(), calls=%async_computation.6 | async-start | bytes 2621440 | tf_op jit(solution)/shard_map/all_gather | solution.py:113
  61.2 33.4 %copy-start.6 = (bf16[3,512,128]{2,1,0:T(8,128)(2,1)S(1)}, bf16[3,512,128]{2,1,0:T(8,128)(2,1)}, u32[]{:S(2)}) copy-start(bf16[3,512,128]{2,1,0:T(8,128)(2,1)} %param.23) | copy-start | bytes 1179652
  61.2 33.4 %copy-start.8 = (f32[512]{0:T(512)S(1)}, f32[512]{0:T(512)}, u32[]{:S(2)}) copy-start(f32[512]{0:T(512)} %param.22) | copy-start | bytes 6148
  61.2 33.4 %copy-start.9 = (f32[512]{0:T(512)S(1)}, f32[512]{0:T(512)}, u32[]{:S(2)}) copy-start(f32[512]{0:T(512)} %param.21) | copy-start | bytes 6148
  70.3 137.9 %all-gather.5.cloned.1.call-start = ((), (), s32[]{:S(2)}) async-start(), calls=%async_computation.3 | async-start | bytes 2621440 | tf_op jit(solution)/shard_map/all_gather | solution.py:122
  183.1 25.1 %copy-start.7 = (bf16[512,128]{1,0:T(8,128)(2,1)S(1)}, bf16[512,128]{1,0:T(8,128)(2,1)}, u32[]{:S(2)}) copy-start(bf16[512,128]{1,0:T(8,128)(2,1)} %param.24) | copy-start | bytes 393220
  183.1 25.1 %copy-start.11 = (f32[128]{0:T(128)S(1)}, f32[128]{0:T(128)}, u32[]{:S(2)}) copy-start(f32[128]{0:T(128)} %param.25) | copy-start | bytes 1540
  185.5 62.3 %all-gather.7.cloned.1.call-start = ((), (), s32[]{:S(2)}) async-start(), calls=%async_computation.4 | async-start | bytes 2621440 | tf_op jit(solution)/shard_map/all_gather | solution.py:141
  189.1 58.7 %copy-start.10 = (f32[512]{0:T(512)S(1)}, f32[512]{0:T(512)}, u32[]{:S(2)}) copy-start(f32[512]{0:T(512)} %param.29) | copy-start | bytes 6148
  224.0 69.0 %copy-start.5 = (f32[128]{0:T(128)S(1)}, f32[128]{0:T(128)}, u32[]{:S(2)}) copy-start(f32[128]{0:T(128)} %param.31) | copy-start | bytes 1540
  224.0 69.0 %reduce-scatter.2.cloned.1.call-start = ((), (), s32[]{:S(2)}) async-start(), calls=%async_computation.5 | async-start | bytes 2621440 | tf_op jit(solution)/shard_map/reduce_scatter | solution.py:147
  295.3 16.4 %copy-start.2 = (s32[3068]{0:T(1024)S(1)}, s32[3068]{0:T(1024)}, u32[]{:S(2)}) copy-start(s32[3068]{0:T(1024)} %get-tuple-element.127) | copy-start | bytes 36820
  307.0 30.3 %all-to-all-start.1 = ((bf16[4,1022,128]{2,1,0:T(8,128)(2,1)}), bf16[4,1022,128]{2,1,0:T(8,128)(2,1)}, u32[]{:S(2)}, u32[]{:S(2)}) async-start(bf16[4,1022,128]{2,1,0:T(8,128)(2,1)} %reshape.72), calls=%async_computation.2 | async-start | bytes 2097152 | tf_op jit(solution)/shard_map/all_to_all | solution.py:152
  339.8 12.4 %copy-start.4 = (pred[3068]{0:T(1024)(128)(4,1)S(1)}, pred[3068]{0:T(1024)(128)(4,1)}, u32[]{:S(2)}) copy-start(pred[3068]{0:T(1024)(128)(4,1)} %copy-done.3) | copy-start | bytes 9208
Sparse Core Ops, SparseCore 0:
  70.4 21.9 all-gather.8
  185.6 22.5 all-gather.4
  224.1 23.6 all-gather.6
  261.7 31.1 reduce-scatter.1
where the time goes:
time: 364 us; the launch traced here: 362 us
  waiting for transfers between devices  134 us (37%)
  local copies, waits for them, and re-layouts  90.1 us (25%)
  matrix products  73.3 us (20%)
  other arithmetic  19.8 us (5%)
  between operations  14.1 us (4%)
  starting transfers between devices  11.1 us (3%)
  blocking collectives  10.2 us (3%)
  loops' own time  9.82 us (3%)
    reduce_scatter x1, waiting for transfers between devices, body(): lax.psum_scatter(partial_down.astype(jnp.bfloat16), 'head', scatter_dimen...  31.3 us
    dot_general x4, matrix products, one_block(): jnp.einsum('hqk,khd->qhd', weights_bf, patch_values, preferred_element_ty...  29.8 us
    all_to_all x1, waiting for transfers between devices, body(): lax.all_to_all(outgoing, 'pts', split_axis=0, concat_axis=0, tiled=True)  25.6 us
    all_gather x1, waiting for transfers between devices, body(): lax.all_gather(normed_cols, 'head', axis=1, tiled=True)  23.7 us
    sub x4, matrix products, one_block(): raised = jnp.exp(scores - jnp.max(scores, axis=2, keepdims=True))  23.3 us
    all_gather x1, waiting for transfers between devices, body(): features = lax.all_gather(feat_cols, 'head', axis=1, tiled=True)  22 us
    scatter x2, local copies, waits for them, and re-layouts, pack_rows(): jnp.zeros((slots_total, width), rows.dtype).at[where_to]  19.7 us
    all_gather x1, waiting for transfers between devices, body(): lax.all_gather(attended, 'head', axis=1, tiled=True)  19.1 us
  transfers between devices with their start and end apart: 6, of which 6 were waited for; matrix products, arithmetic and copies ran while one was open for 5% of the time, Pallas kernels for 0%

commit v1 on v0

v1 whole, which is shorter than its diff:
```python
import functools
import math

import jax
import jax.numpy as jnp
from jax import lax
from jax.experimental import pallas as pl
from jax.experimental.pallas import tpu as pltpu
from jax.sharding import PartitionSpec as P

PATCH = 1024
HEAD_DIM = 16
LANES = 128
F32 = jnp.float32
BF = jnp.bfloat16
I32 = jnp.int32
SMEM = pl.BlockSpec(memory_space=pltpu.SMEM)
VMEM = pl.BlockSpec(memory_space=pltpu.VMEM)
ANY = pl.BlockSpec(memory_space=pl.ANY)


def dot(lhs, rhs, dims=(1, 0)):
    return lax.dot_general(
        lhs, rhs, (((dims[0],), (dims[1],)), ((), ())), preferred_element_type=F32
    )


def round_up(value, unit):
    return (value + unit - 1) // unit * unit


def copies_in(sources, targets, sems):
    copies = [
        pltpu.make_async_copy(source, target, sems.at[i])
        for i, (source, target) in enumerate(zip(sources, targets))
    ]
    for copy in copies:
        copy.start()
    return copies


def convert_rows(source, source_at, target, target_at, rows, step):
    def one(i, carry):
        at = pl.multiple_of(i * step, step)
        target[pl.ds(target_at + at, step), :] = source[pl.ds(source_at + at, step), :].astype(
            target.dtype
        )
        return carry

    lax.fori_loop(0, rows // step, one, 0, unroll=2)


def pack_kernel(
    shards, cap, rows_here, columns_at, meta, rank, z_feat, *refs
):
    sends = refs[:shards]
    place_out = refs[shards]
    place, place_smem, narrow, wide, packed, sems = refs[shards + 1 :]
    here, count = meta[0], meta[2]
    slots = place.shape[1]
    zone_rows, width = narrow.shape
    if columns_at:
        column = pl.multiple_of(meta[1] * width, width)
        source = z_feat.at[:, pl.ds(column, width)]
    else:
        source = z_feat
    feature_copy = pltpu.make_async_copy(source, narrow, sems.at[0])
    feature_copy.start()

    grid_rows = shards * rows_here // LANES
    block = rows_here // LANES
    ranks = rank[...]
    occupied = lax.broadcasted_iota(I32, (1, slots), 1) < count
    major = jnp.where(occupied, ranks // LANES, -1)
    minor = ranks % LANES
    hot_major = (lax.broadcasted_iota(I32, (grid_rows, slots), 0) == major).astype(BF)
    hot_minor = (lax.broadcasted_iota(I32, (LANES, slots), 0) == minor).astype(BF)
    members = dot(hot_minor, hot_major, (1, 1)).astype(BF)
    minor_r = lax.broadcasted_iota(I32, (LANES, LANES), 0)
    minor_c = lax.broadcasted_iota(I32, (LANES, LANES), 1)
    below = (minor_c < minor_r).astype(BF)
    major_r = lax.broadcasted_iota(I32, (grid_rows, grid_rows), 0)
    major_c = lax.broadcasted_iota(I32, (grid_rows, grid_rows), 1)
    earlier = ((major_r < major_c) & (major_r // block == major_c // block)).astype(BF)
    row_wise = dot(members, earlier)
    counts = dot(below, members) + dot(jnp.ones((LANES, LANES), BF), row_wise.astype(BF))
    high = jnp.floor(counts * (1.0 / 32.0))
    low = counts - high * 32.0
    spread = dot(high.astype(BF), hot_major) * 32.0 + dot(low.astype(BF), hot_major)
    found = jnp.sum(jnp.where(hot_minor > 0, spread, 0.0), axis=0, keepdims=True)
    target = ranks // rows_here
    place[...] = jnp.where(occupied, target * cap + found.astype(I32), shards * cap)
    to_smem = pltpu.make_async_copy(place, place_smem, sems.at[1])
    to_smem.start()
    to_out = pltpu.make_async_copy(place, place_out, sems.at[2])
    to_out.start()
    feature_copy.wait()
    whole_rows = zone_rows // 16 * 16
    convert_rows(narrow, 0, wide, 0, whole_rows, 16)
    if whole_rows < zone_rows:
        wide[pl.ds(whole_rows, zone_rows - whole_rows), :] = narrow[
            pl.ds(whole_rows, zone_rows - whole_rows), :
        ].astype(F32)
    to_smem.wait()

    def place_rows(i, carry):
        base = pl.multiple_of(i * 8, 8)
        for k in range(8):
            packed[pl.ds(place_smem[0, base + k], 1), :] = wide[pl.ds(base + k, 1), :]
        return carry

    lax.fori_loop(0, (count + 7) // 8, place_rows, 0)
    for k in range(shards):
        at = pl.multiple_of(lax.rem(here + k, shards) * cap, cap)
        convert_rows(packed, at, sends[k], 0, cap, 16)
    to_out.wait()


def pack(meta, rank, z_feat, columns_at, width, shards, cap, rows_here):
    zone_rows = z_feat.shape[0]
    slots = rank.shape[1]
    return pl.pallas_call(
        functools.partial(pack_kernel, shards, cap, rows_here, columns_at),
        out_shape=[jax.ShapeDtypeStruct((cap, width), BF)] * shards
        + [jax.ShapeDtypeStruct((1, slots), I32)],
        in_specs=[SMEM, VMEM, ANY],
        out_specs=[VMEM] * shards + [ANY],
        scratch_shapes=[
            pltpu.VMEM((1, slots), I32),
            pltpu.SMEM((1, slots), I32),
            pltpu.VMEM((zone_rows, width), BF),
            pltpu.VMEM((slots, width), F32),
            pltpu.VMEM((shards * cap + 8, width), F32),
            pltpu.SemaphoreType.DMA((3,)),
        ],
        name="pack",
    )(meta, rank, z_feat)


def move_segment(source, source_at, target, target_at, length):
    def one(i, carry):
        for k in range(4):
            target[pl.ds(target_at + i * 32 + k * 8, 8), :] = source[
                pl.ds(source_at + i * 32 + k * 8, 8), :
            ]
        return carry

    lax.fori_loop(0, (length + 31) // 32, one, 0)


def segment_starts(pieces, patches, shards, cap):
    packed_at, patch_at = {}, {}
    for s in range(shards):
        at = s * cap
        for p in range(patches):
            packed_at[p, s] = at
            at = at + pieces[p, s]
    for p in range(patches):
        at = p * PATCH
        for s in range(shards):
            patch_at[p, s] = at
            at = at + pieces[p, s]
    return packed_at, patch_at


def compact_kernel(shards, patches, group, cap, meta, pieces, *refs):
    blocks = refs[:shards]
    outs = refs[shards : shards + patches]
    narrow, wide, patch_rows, sems = refs[shards + patches :]
    here, member = meta[0], meta[1]
    sources = [lax.rem(here - k + shards, shards) for k in range(shards)]
    arrivals = copies_in(blocks, [narrow.at[s] for s in sources], sems)
    for copy in arrivals:
        copy.wait()
    for s in range(shards):
        convert_rows(narrow.at[s], 0, wide, s * cap, cap, 16)
    packed_at, patch_at = segment_starts(pieces, patches, shards, cap)
    for p in range(patches):
        for s in range(shards):
            move_segment(wide, packed_at[p, s], patch_rows, patch_at[p, s], pieces[p, s])
    own_group = member // group
    for k in range(patches):
        at = pl.multiple_of(lax.rem(own_group + k, patches) * PATCH, PATCH)
        convert_rows(patch_rows, at, outs[k], 0, PATCH, 16)


def compact(meta, pieces, blocks, patches, group):
    shards = len(blocks)
    cap, width = blocks[0].shape
    return pl.pallas_call(
        functools.partial(compact_kernel, shards, patches, group, cap),
        out_shape=[jax.ShapeDtypeStruct((PATCH, width), BF)] * patches,
        in_specs=[SMEM, SMEM] + [ANY] * shards,
        out_specs=[VMEM] * patches,
        scratch_shapes=[
            pltpu.VMEM((shards, cap, width), BF),
            pltpu.VMEM((shards * cap + 64, width), F32),
            pltpu.VMEM((patches * PATCH + 64, width), F32),
            pltpu.SemaphoreType.DMA((shards,)),
        ],
        name="compact",
    )(meta, pieces, *blocks)


def spread_kernel(shards, patches, members, cap, meta, pieces, *refs):
    blocks = refs[:members]
    sends = refs[members : members + shards]
    narrow, patch_rows, wide, sems = refs[members + shards :]
    here, member = meta[0], meta[1]
    part_rows = narrow.shape[1]
    sources = [lax.rem(member - k + members, members) for k in range(members)]
    arrivals = copies_in(blocks, [narrow.at[s] for s in sources], sems)
    for copy in arrivals:
        copy.wait()
    for s in range(members):
        convert_rows(narrow.at[s], 0, patch_rows, s * part_rows, part_rows, 16)
    packed_at, patch_at = segment_starts(pieces, patches, shards, cap)
    for s in range(shards):
        for p in range(patches):
            move_segment(patch_rows, patch_at[p, s], wide, packed_at[p, s], pieces[p, s])
    for k in range(shards):
        at = pl.multiple_of(lax.rem(here + k, shards) * cap, cap)
        convert_rows(wide, at, sends[k], 0, cap, 16)


def spread(meta, pieces, blocks, patches, shards, cap):
    members = len(blocks)
    part_rows, width = blocks[0].shape
    return pl.pallas_call(
        functools.partial(spread_kernel, shards, patches, members, cap),
        out_shape=[jax.ShapeDtypeStruct((cap, width), BF)] * shards,
        in_specs=[SMEM, SMEM] + [ANY] * members,
        out_specs=[VMEM] * shards,
        scratch_shapes=[
            pltpu.VMEM((members, part_rows, width), BF),
            pltpu.VMEM((patches * PATCH + 64, width), F32),
            pltpu.VMEM((shards * cap + 64, width), F32),
            pltpu.SemaphoreType.DMA((members,)),
        ],
        name="spread",
    )(meta, pieces, *blocks)


def unpack_kernel(shards, cap, meta, place, *refs):
    blocks = refs[:shards]
    out = refs[shards]
    narrow, wide, picked, sems = refs[shards + 1 :]
    here, count = meta[0], meta[2]
    zone_rows, width = out.shape
    sources = [lax.rem(here - k + shards, shards) for k in range(shards)]
    arrivals = copies_in(blocks, [narrow.at[s] for s in sources], sems)
    for copy in arrivals:
        copy.wait()
    for s in range(shards):
        convert_rows(narrow.at[s], 0, wide, s * cap, cap, 16)

    def pick_rows(i, carry):
        base = pl.multiple_of(i * 8, 8)
        for k in range(8):
            picked[pl.ds(base + k, 1), :] = wide[pl.ds(place[0, base + k], 1), :]
        return carry

    lax.fori_loop(0, (count + 7) // 8, pick_rows, 0)

    def masked(at, rows):
        slot = at + lax.broadcasted_iota(I32, (rows, width), 0)
        out[pl.ds(at, rows), :] = jnp.where(slot < count, picked[pl.ds(at, rows), :], 0.0).astype(
            BF
        )

    def one(i, carry):
        masked(pl.multiple_of(i * 16, 16), 16)
        return carry

    whole_rows = zone_rows // 16 * 16
    lax.fori_loop(0, whole_rows // 16, one, 0, unroll=2)
    if whole_rows < zone_rows:
        masked(whole_rows, zone_rows - whole_rows)


def unpack(meta, place, blocks, zone_rows):
    shards = len(blocks)
    cap, width = blocks[0].shape
    slots = place.shape[1]
    return pl.pallas_call(
        functools.partial(unpack_kernel, shards, cap),
        out_shape=jax.ShapeDtypeStruct((zone_rows, width), BF),
        in_specs=[SMEM, SMEM] + [ANY] * shards,
        out_specs=VMEM,
        scratch_shapes=[
            pltpu.VMEM((shards, cap, width), BF),
            pltpu.VMEM((shards * cap + 8, width), F32),
            pltpu.VMEM((slots, width), F32),
            pltpu.SemaphoreType.DMA((shards,)),
        ],
        name="unpack",
    )(meta, place, *blocks)


def row_stats(parts, width):
    total = jnp.sum(sum(parts[1:], parts[0]), axis=1, keepdims=True)
    squares = jnp.sum(
        sum((x * x for x in parts[1:]), parts[0] * parts[0]), axis=1, keepdims=True
    )
    mean = total / width
    var = squares / width - mean * mean
    return mean, lax.rsqrt(var + 1e-05)


def attend_kernel(blocks, queries, chunk, ids, gain, bias, *refs):
    feats = refs[:blocks]
    weights = refs[blocks : 2 * blocks]
    out, kept = refs[2 * blocks : 2 * blocks + 2]
    features, weight, normed, keys, query, mixed, sems = refs[2 * blocks + 2 :]
    rows = features.shape[1]
    width = blocks * LANES
    places = [ids[k] for k in range(blocks)]
    feature_copies = copies_in(feats, [features.at[k] for k in places], sems)
    weight_copies = copies_in(weights, [weight.at[k] for k in places], sems.at[pl.ds(blocks, blocks)])
    for copy in feature_copies:
        copy.wait()
    first = pl.multiple_of(ids[blocks] * queries, queries)

    def norm(i, carry):
        at = pl.ds(pl.multiple_of(i * 128, 128), 128)
        parts = [features[b, at, :].astype(F32) for b in range(blocks)]
        mean, scale = row_stats(parts, width)
        for b in range(blocks):
            cols = slice(b * LANES, (b + 1) * LANES)
            normed[at, cols] = (
                (parts[b] - mean) * scale * gain[0:1, cols] + bias[0:1, cols]
            ).astype(BF)
        return carry

    lax.fori_loop(0, rows // 128, norm, 0, unroll=2)
    for b in range(blocks):
        kept[b] = features[b, pl.ds(first, queries), :]
    for copy in weight_copies:
        copy.wait()
    lane = lax.broadcasted_iota(I32, (1, LANES), 1)
    keys[:, 2 * LANES :] = jnp.ones((rows, LANES), BF)
    score_scale = HEAD_DIM ** (-0.5) * math.log2(math.e)

    def one_block(b, carry):
        key_value = jnp.concatenate([weight[b, 1], weight[b, 2]], axis=1)
        for i in range(rows // 256):
            at = pl.ds(i * 256, 256)
            keys[at, : 2 * LANES] = dot(normed[at, :], key_value).astype(BF)
        for i in range(queries // chunk):
            at = pl.ds(pl.multiple_of(first + i * chunk, chunk), chunk)
            query[pl.ds(i * chunk, chunk), :] = (
                dot(normed[at, :], weight[b, 0]) * score_scale
            ).astype(BF)

        def one_head(j, carry):
            mask = lane // HEAD_DIM == j
            for i in range(queries // chunk):
                at = pl.ds(i * chunk, chunk)
                own = jnp.where(mask, query[at, :], jnp.zeros((), BF))
                scores = dot(own, keys[:, :LANES], (1, 1))
                raised = jnp.exp2(scores - jnp.max(scores, axis=1, keepdims=True)).astype(BF)
                summed = dot(raised, keys[:, LANES:])
                mixed[at, :] = jnp.where(
                    mask, summed[:, :LANES] / summed[:, LANES:], mixed[at, :]
                )
            return carry

        lax.fori_loop(0, LANES // HEAD_DIM, one_head, 0)
        out[b] = mixed[...].astype(BF)
        return carry

    lax.fori_loop(0, blocks, one_block, 0)


def attend(ids, feats, weights, gain, bias, queries):
    blocks = len(feats)
    rows = feats[0].shape[0]
    width = weights[0].shape[1]
    chunk = min(128, queries)
    flops = 4 * queries * rows * LANES * blocks * (LANES // HEAD_DIM)
    return pl.pallas_call(
        functools.partial(attend_kernel, blocks, queries, chunk),
        out_shape=[jax.ShapeDtypeStruct((blocks, queries, LANES), BF)] * 2,
        in_specs=[SMEM, VMEM, VMEM] + [ANY] * (2 * blocks),
        out_specs=[VMEM, VMEM],
        scratch_shapes=[
            pltpu.VMEM((blocks, rows, LANES), BF),
            pltpu.VMEM((blocks, 3, width, LANES), BF),
            pltpu.VMEM((rows, width), BF),
            pltpu.VMEM((rows, 3 * LANES), BF),
            pltpu.VMEM((queries, LANES), BF),
            pltpu.VMEM((queries, LANES), F32),
            pltpu.SemaphoreType.DMA((2 * blocks,)),
        ],
        cost_estimate=pl.CostEstimate(
            flops=flops, bytes_accessed=4 * rows * width, transcendentals=0
        ),
        name="attend",
    )(ids, gain, bias, *feats, *weights)


def mlp_kernel(blocks, members, sends, chunk, ids, gain, bias, mixed, kept, *refs):
    projs = refs[:blocks]
    ups = refs[blocks : blocks + members]
    downs = refs[blocks + members : blocks + 2 * members]
    vectors = refs[blocks + 2 * members : blocks + 3 * members]
    results = refs[blocks + 3 * members : blocks + 3 * members + sends]
    proj, up, down, vector, final, sems = refs[blocks + 3 * members + sends :]
    rows = mixed.shape[1]
    width = blocks * LANES
    hidden_here = up.shape[2]
    share = width // members
    spots = [ids[blocks + 1 + k] for k in range(members)]
    copies = copies_in(projs, [proj.at[ids[k]] for k in range(blocks)], sems)
    copies += copies_in(
        vectors, [vector.at[k] for k in spots], sems.at[pl.ds(blocks, members)]
    )
    late = copies_in(
        ups, [up.at[k] for k in range(members)], sems.at[pl.ds(blocks + members, members)]
    )
    late += copies_in(
        downs, [down.at[k] for k in range(members)], sems.at[pl.ds(blocks + 2 * members, members)]
    )
    for copy in copies:
        copy.wait()
    for copy in late:
        copy.wait()
    out_bias = jnp.concatenate([vector[k, :, :share] for k in range(members)], axis=1)
    down_bias = jnp.concatenate([vector[k, :, share : 2 * share] for k in range(members)], axis=1)
    out_weight = jnp.concatenate([proj[b] for b in range(blocks)], axis=1)
    root_half = 0.5 ** 0.5

    def one(i, carry):
        at = pl.ds(pl.multiple_of(i * chunk, chunk), chunk)
        attended = jnp.concatenate([mixed[b, at, :] for b in range(blocks)], axis=1)
        features = jnp.concatenate([kept[b, at, :] for b in range(blocks)], axis=1)
        residual = (features.astype(F32) + dot(attended, out_weight) + out_bias).astype(BF)
        wide = residual.astype(F32)
        mean, scale = row_stats([wide], width)
        normed = ((wide - mean) * scale * gain[...] + bias[...]).astype(BF)
        total = wide + down_bias
        for k in range(members):
            spot = spots[k]
            before = dot(normed, up[k]) + vector[spot, :, 2 * share :]
            hidden = (0.5 * before * (1.0 + lax.erf(before * root_half))).astype(BF)
            total = total + dot(hidden, down[k])
        for b in range(blocks):
            final[b, at, :] = total[:, b * LANES : (b + 1) * LANES].astype(BF)
        return carry

    lax.fori_loop(0, rows // chunk, one, 0)
    if sends > 1:
        me = ids[blocks + 1]
        for k in range(sends):
            results[k][...] = final[lax.rem(me + k, sends)]
    else:
        results[0][...] = final[...]


def mlp(ids, gain, bias, mixed, kept, projs, ups, downs, vectors):
    blocks, rows, _ = mixed.shape
    members = len(ups)
    width = blocks * LANES
    hidden_here = ups[0].shape[1]
    sends = members if members == blocks else 1
    shape = (rows, LANES) if sends > 1 else (blocks, rows, LANES)
    chunk = min(256, rows)
    return pl.pallas_call(
        functools.partial(mlp_kernel, blocks, members, sends, chunk),
        out_shape=[jax.ShapeDtypeStruct(shape, BF)] * sends,
        in_specs=[SMEM, VMEM, VMEM, VMEM, VMEM] + [ANY] * (blocks + 3 * members),
        out_specs=[VMEM] * sends,
        scratch_shapes=[
            pltpu.VMEM((blocks, width, LANES), BF),
            pltpu.VMEM((members, width, hidden_here), BF),
            pltpu.VMEM((members, hidden_here, width), BF),
            pltpu.VMEM((members, 1, vectors[0].shape[1]), F32),
            pltpu.VMEM((blocks, rows, LANES), BF),
            pltpu.SemaphoreType.DMA((blocks + 3 * members,)),
        ],
        cost_estimate=pl.CostEstimate(
            flops=4 * rows * width * hidden_here * members,
            bytes_accessed=4 * width * hidden_here * members,
            transcendentals=0,
        ),
        name="mlp",
    )(ids, gain, bias, mixed, kept, *projs, *ups, *downs, *vectors)


def shift(array, axis, size, step):
    return lax.ppermute(array, axis, [(i, (i + step) % size) for i in range(size)])


def exchange(blocks, axis, size):
    if size <= 8:
        return [blocks[0]] + [shift(blocks[k], axis, size, k) for k in range(1, size)]
    me = lax.axis_index(axis)
    steps = jnp.arange(size, dtype=I32)
    stacked = jnp.stack(blocks)[(steps - me) % size]
    got = lax.all_to_all(stacked, axis, 0, 0, tiled=True)[(me - steps) % size]
    return [got[k] for k in range(size)]


def gather_members(array, groups, group):
    size = groups * group
    found = []
    for k in range(groups):
        pairs = [(i, (i // group + k) % groups * group + i % group) for i in range(size)]
        moved = array if k == 0 else lax.ppermute(array, "head", pairs)
        for j in range(group):
            pairs = [(i, i // group * group + (i % group + j) % group) for i in range(size)]
            found.append(moved if j == 0 else lax.ppermute(moved, "head", pairs))
    return found


def body(
    z_feat,
    shard_count,
    hilbert_rank,
    z_slot,
    ln1_gain,
    ln1_bias,
    w_qkv,
    w_out,
    b_out,
    ln2_gain,
    ln2_bias,
    w_up,
    b_up,
    w_down,
    b_down,
):
    shards = lax.axis_size("pts")
    members = lax.axis_size("head")
    rows_here = z_slot.shape[0]
    zone_rows, full_width = z_feat.shape
    width = w_out.shape[1]
    patches = rows_here // PATCH
    group = members // patches
    queries = PATCH // group
    blocks = full_width // LANES
    skew_step = rows_here // (2 * shards * (shards - 1))
    cap = round_up(rows_here // shards + 2 * skew_step * (shards - 1), 16)
    here = lax.axis_index("pts")
    member = lax.axis_index("head")
    meta = jnp.stack([here, member, shard_count[0]]).astype(I32)

    order = [
        (member // group - k) % patches * group + (member % group - j) % group
        for k in range(patches)
        for j in range(group)
    ]
    spots = jnp.stack(order).astype(I32)
    part = (member % group).astype(I32)[None]

    def natural(found):
        stacked = jnp.stack(found)
        back = jnp.zeros((members,), I32).at[spots].set(jnp.arange(members, dtype=I32))
        stacked = jnp.take(stacked, back, axis=0)
        joined = jnp.concatenate([stacked[i] for i in range(members)], axis=-1)
        return [joined[..., b * LANES : (b + 1) * LANES] for b in range(blocks)]

    qkv_found = gather_members(w_qkv, patches, group)
    out_found = gather_members(w_out, patches, group)
    up_found = gather_members(w_up, patches, group)
    down_found = gather_members(w_down, patches, group)
    vectors = gather_members(
        jnp.concatenate([b_out, b_down, b_up])[None, :], patches, group
    )

    slots = round_up(zone_rows, LANES)
    rank = jnp.pad(hilbert_rank, (0, slots - zone_rows))[None, :]
    if width % LANES == 0:
        z_source = z_feat
    else:
        z_source = lax.dynamic_slice_in_dim(z_feat, member * width, width, 1)
    *sends, place = pack(
        meta, rank, z_source, width % LANES == 0, width, shards, cap, rows_here
    )
    source = (z_slot // zone_rows).reshape(patches, PATCH, 1)
    pieces = jnp.sum((source == jnp.arange(shards, dtype=I32)).astype(I32), axis=1)
    arrived = exchange(sends, "pts", shards)
    patch_blocks = compact(meta, pieces, arrived, patches, group)
    feats = []
    for k in range(patches):
        pairs = [(i, (i // group + k) % patches * group + i % group) for i in range(members)]
        moved = patch_blocks[k] if k == 0 else lax.ppermute(patch_blocks[k], "head", pairs)
        for j in range(group):
            pairs = [(i, i // group * group + (i % group + j) % group) for i in range(members)]
            feats.append(moved if j == 0 else lax.ppermute(moved, "head", pairs))

    if width == LANES:
        block_ids = spots
        qkv_blocks, out_blocks = qkv_found, out_found
    else:
        block_ids = jnp.arange(blocks, dtype=I32)
        feats = natural(feats)
        qkv_blocks, out_blocks = natural(qkv_found), natural(out_found)
    ids = jnp.concatenate([block_ids, part, spots])

    mixed, kept = attend(
        ids, feats, qkv_blocks, ln1_gain[None, :], ln1_bias[None, :], queries
    )
    results = mlp(
        ids,
        ln2_gain[None, :],
        ln2_bias[None, :],
        mixed,
        kept,
        out_blocks,
        up_found,
        down_found,
        vectors,
    )
    if width != LANES:
        joined = jnp.concatenate([results[0][b] for b in range(blocks)], axis=1)
        results = [
            lax.dynamic_slice_in_dim(joined, (member + k) % members * width, width, 1)
            for k in range(members)
        ]
    parts = [results[0]] + [shift(results[k], "head", members, k) for k in range(1, members)]
    outgoing = spread(meta, pieces, parts, patches, shards, cap)
    returned = exchange(outgoing, "pts", shards)
    return unpack(meta, place, returned, zone_rows)


def solution(mesh):
    placed = (
        P(("tile", "pts"), None),
        P(("tile", "pts")),
        P(("tile", "pts")),
        P(("tile", "pts")),
        P(),
        P(),
        P(None, None, "head"),
        P(None, "head"),
        P("head"),
        P(),
        P(),
        P(None, "head"),
        P("head"),
        P("head", None),
        P("head"),
    )
    return jax.shard_map(
        body, mesh=mesh, in_specs=placed, out_specs=P(("tile", "pts"), "head"), check_vma=False
    )
```

time: 364 us -> 175 us (0.48)
  the two profiles are of different devices: /device:TPU:0 before, /device:TPU:15 now
where the time goes in v1:
time: 175 us
  Pallas kernels  73.4 us (42%)
  waiting for transfers between devices  61.7 us (35%)
  starting transfers between devices  32.7 us (19%)
  local copies, waits for them, and re-layouts  4.31 us (2%)
    pallas_call x1, Pallas kernels, attend(): pl.pallas_call(functools.partial(attend_kernel, blocks, queries, chunk),...  39.4 us
    ppermute x9, waiting for transfers between devices, shift(): lax.ppermute(array, axis, [(i, (i + step) % size) for i in range(size)])  32.9 us
    ppermute x1, waiting for transfers between devices, body(): lax.ppermute(patch_blocks[k], 'head', pairs)  26.7 us
    ppermute x10, starting transfers between devices, gather_members(): found.append(moved if j == 0 else lax.ppermute(moved, 'head', pairs))  18.2 us
    ppermute x9, starting transfers between devices, shift(): lax.ppermute(array, axis, [(i, (i + step) % size) for i in range(size)])  9.99 us
    pallas_call x1, Pallas kernels, mlp(): pl.pallas_call(functools.partial(mlp_kernel, blocks, members, sends, chun...  8.84 us
    pallas_call x1, Pallas kernels, pack(): pl.pallas_call(functools.partial(pack_kernel, shards, cap, rows_here, col...  8.01 us
    pallas_call x1, Pallas kernels, unpack(): pl.pallas_call(functools.partial(unpack_kernel, shards, cap), out_shape=j...  7.81 us
  transfers between devices with their start and end apart: 27, of which 12 were waited for; matrix products, arithmetic and copies ran while one was open for 1% of the time, Pallas kernels for 25%

profile of v1, /device:TPU:15, one launch (start us, length us, event | category | flops | bytes accessed | tf_op | source)
XLA Modules:
  0.0 174.6 jit_solution(16072623521036987190)
XLA Ops:
  0.8 1.3 pad.4
  2.7 8.0 %pack.1 = (bf16[1024,128]{1,0:T(8,128)(2,1)}, bf16[1024,128]{1,0:T(8,128)(2,1)}, bf16[1024,128]{1,0:T(8,128)(2,1)}, bf16[1024,128]{1,0:T(8,128)(2,1)}, s32[1,3072]{1,0:T(1,128)}) custom-call(s32[3]{0:T(128)} %pad_add_fusion.meta, s32[1,3072]{1,0:T(1,128)} %bitcast.12, bf16[3068,512]{1,0:T(8,128)(2,1)} %z_feat.1), custom_call_target="tpu_custom_call" | custom-call | tf_op jit(solution)/shard_map/pack/pallas_call | solution.py:122
  10.7 2.2 %collective-permute-start = (bf16[1024,128]{1,0:T(8,128)(2,1)}, bf16[1024,128]{1,0:T(8,128)(2,1)S(1)}, u32[]{:S(2)}, u32[]{:S(2)}) collective-permute-start(bf16[1024,128]{1,0:T(8,128)(2,1)} %get-tuple-element.24), channel_id=1, source_target_pairs={{0,4},{4,8},{8,12},{12,0},{1,5},{5,9},{9,13},{13,1},{2,6},{6,10},{... | collective-permute-start | bytes 786440 | tf_op jit(solution)/shard_map/ppermute | solution.py:491
  12.9 1.3 collective-permute-start.2
  14.2 1.3 collective-permute-start.18
  16.7 1.6 collective-permute-done.19.refs_14_
  18.7 13.4 %collective-permute-start.9 = (bf16[512,128]{1,0:T(8,128)(2,1)S(1)}, bf16[512,128]{1,0:T(8,128)(2,1)}, u32[]{:S(2)}, u32[]{:S(2)}) collective-permute-start(bf16[512,128]{1,0:T(8,128)(2,1)S(1)} %copy-done.23), channel_id=1, source_target_pairs={{0,1},{1,0},{2,3},{3,2},{4,5},{5,4},{6,7},{7,6},{8,9},{9,8},{10,11... | collective-permute-start | bytes 393224 | tf_op jit(solution)/shard_map/ppermute | solution.py:512
  32.1 3.0 %collective-permute-done.1.refs_2_ = bf16[1024,128]{1,0:T(8,128)(2,1)S(1)} collective-permute-done((bf16[1024,128]{1,0:T(8,128)(2,1)}, bf16[1024,128]{1,0:T(8,128)(2,1)S(1)}, u32[]{:S(2)}, u32[]{:S(2)}) %collective-permute-start.1) | collective-permute-done | bytes 262176 | tf_op jit(solution)/shard_map/ppermute | solution.py:491
  35.4 0.7 collective-permute-done.2.refs_3_
  36.1 1.2 collective-permute-start.20
  37.3 0.7 convert_reduce_fusion.pieces
  38.0 4.7 %compact.1 = (bf16[1024,128]{1,0:T(8,128)(2,1)}, bf16[1024,128]{1,0:T(8,128)(2,1)}) custom-call(s32[3]{0:T(128)} %pad_add_fusion.meta, s32[2,4]{1,0:T(2,128)} %convert_reduce_fusion.pieces, bf16[1024,128]{1,0:T(8,128)(2,1)} %get-tuple-element.23.refs_0_, bf16[1024,128]{1,0:T(8,128)(2,1)} %copy-done, bf16[1024,128]{1,0:T(8,128)(2,1)} %copy-done.1, ...), custom_call_target="tpu_custom_call" | custom-call | tf_op jit(solution)/shard_map/compact/pallas_call | solution.py:190
  42.7 1.3 collective-permute-start.13
  44.3 1.2 collective-permute-start.4
  45.5 0.9 collective-permute-start.8
  46.4 26.7 %collective-permute-done.4.refs_2_ = bf16[1024,128]{1,0:T(8,128)(2,1)S(1)} collective-permute-done((bf16[1024,128]{1,0:T(8,128)(2,1)}, bf16[1024,128]{1,0:T(8,128)(2,1)S(1)}, u32[]{:S(2)}, u32[]{:S(2)}) %collective-permute-start.4) | collective-permute-done | bytes 262176 | tf_op jit(solution)/shard_map/ppermute | solution.py:587
  73.1 0.9 collective-permute-start.5
  75.8 39.4 %attend.1 = (bf16[4,512,128]{2,1,0:T(8,128)(2,1)}, bf16[4,512,128]{2,1,0:T(8,128)(2,1)}) custom-call(s32[9]{0:T(128)} %concatenate.7.ids, f32[1,512]{1,0:T(1,128)} %bitcast.13, f32[1,512]{1,0:T(1,128)} %bitcast.14, bf16[1024,128]{1,0:T(8,128)(2,1)} %get-tuple-element.27.refs_0_, bf16[1024,128]{1,0:T(8,128)(2,1)} %collective-permute-done.3.refs_1_, ...), custom_call_target="tpu_custom_call" | custom-call | flops 8589934592 | bytes 2097152 | tf_op jit(solution)/shard_map/attend/pallas_call | solution.py:381
  115.3 0.7 copy-done.18
  116.3 8.8 %mlp.1 = (bf16[512,128]{1,0:T(8,128)(2,1)}, bf16[512,128]{1,0:T(8,128)(2,1)}, bf16[512,128]{1,0:T(8,128)(2,1)}, bf16[512,128]{1,0:T(8,128)(2,1)}) custom-call(s32[9]{0:T(128)} %concatenate.7.ids, f32[1,512]{1,0:T(1,128)} %bitcast.15, f32[1,512]{1,0:T(1,128)} %bitcast.16, bf16[4,512,128]{2,1,0:T(8,128)(2,1)} %get-tuple-element.29.mixed, ...), custom_call_target="tpu_custom_call" | custom-call | flops 2147483648 | bytes 4194304 | tf_op jit(solution)/shard_map/mlp/pallas_call | solution.py:468
  125.1 1.6 collective-permute-start.21
  127.2 2.5 %collective-permute-done.21.refs_1_ = bf16[512,128]{1,0:T(8,128)(2,1)S(1)} collective-permute-done((bf16[512,128]{1,0:T(8,128)(2,1)}, bf16[512,128]{1,0:T(8,128)(2,1)S(1)}, u32[]{:S(2)}, u32[]{:S(2)}) %collective-permute-start.21) | collective-permute-done | bytes 131104 | tf_op jit(solution)/shard_map/ppermute | solution.py:491
  129.6 3.4 %collective-permute-done.22.refs_2_ = bf16[512,128]{1,0:T(8,128)(2,1)S(1)} collective-permute-done((bf16[512,128]{1,0:T(8,128)(2,1)}, bf16[512,128]{1,0:T(8,128)(2,1)S(1)}, u32[]{:S(2)}, u32[]{:S(2)}) %collective-permute-start.22) | collective-permute-done | bytes 131104 | tf_op jit(solution)/shard_map/ppermute | solution.py:491
  133.0 0.7 collective-permute-done.23.refs_3_
  134.3 4.7 %spread.1 = (bf16[1024,128]{1,0:T(8,128)(2,1)}, bf16[1024,128]{1,0:T(8,128)(2,1)}, bf16[1024,128]{1,0:T(8,128)(2,1)}, bf16[1024,128]{1,0:T(8,128)(2,1)}) custom-call(s32[3]{0:T(128)} %pad_add_fusion.meta, s32[2,4]{1,0:T(2,128)} %convert_reduce_fusion.pieces, bf16[512,128]{1,0:T(8,128)(2,1)} %get-tuple-element.31.refs_0_, bf16[512,128]{1,0:T(8,128)(2,1)} %copy-done.6, ...), custom_call_target="tpu_custom_call" | custom-call | tf_op jit(solution)/shard_map/spread/pallas_call | solution.py:229
  139.2 3.0 %collective-permute-start.25 = (bf16[1024,128]{1,0:T(8,128)(2,1)}, bf16[1024,128]{1,0:T(8,128)(2,1)S(1)}, u32[]{:S(2)}, u32[]{:S(2)}) collective-permute-start(bf16[1024,128]{1,0:T(8,128)(2,1)} %get-tuple-element.37), channel_id=1, source_target_pairs={{0,8},{4,12},{8,0},{12,4},{1,9},{5,13},{9,1},{13,5},{2,10},{6,14},... | collective-permute-start | bytes 786440 | tf_op jit(solution)/shard_map/ppermute | solution.py:491
  142.2 1.4 collective-permute-start.26
  143.6 3.8 %collective-permute-done.24.refs_1_ = bf16[1024,128]{1,0:T(8,128)(2,1)S(1)} collective-permute-done((bf16[1024,128]{1,0:T(8,128)(2,1)}, bf16[1024,128]{1,0:T(8,128)(2,1)S(1)}, u32[]{:S(2)}, u32[]{:S(2)}) %collective-permute-start.24) | collective-permute-done | bytes 262176 | tf_op jit(solution)/shard_map/ppermute | solution.py:491
  147.4 15.0 %collective-permute-done.25.refs_2_ = bf16[1024,128]{1,0:T(8,128)(2,1)S(1)} collective-permute-done((bf16[1024,128]{1,0:T(8,128)(2,1)}, bf16[1024,128]{1,0:T(8,128)(2,1)S(1)}, u32[]{:S(2)}, u32[]{:S(2)}) %collective-permute-start.25) | collective-permute-done | bytes 262176 | tf_op jit(solution)/shard_map/ppermute | solution.py:491
  162.4 3.6 %collective-permute-done.26.refs_3_ = bf16[1024,128]{1,0:T(8,128)(2,1)S(1)} collective-permute-done((bf16[1024,128]{1,0:T(8,128)(2,1)}, bf16[1024,128]{1,0:T(8,128)(2,1)S(1)}, u32[]{:S(2)}, u32[]{:S(2)}) %collective-permute-start.26) | collective-permute-done | bytes 262176 | tf_op jit(solution)/shard_map/ppermute | solution.py:491
  166.0 0.7 copy-done.5
  166.7 7.8 %unpack.1 = bf16[3068,128]{1,0:T(8,128)(2,1)} custom-call(s32[3]{0:T(128)} %pad_add_fusion.meta, s32[1,3072]{1,0:T(1,128)} %get-tuple-element.22.place, bf16[1024,128]{1,0:T(8,128)(2,1)} %get-tuple-element.35.refs_0_, bf16[1024,128]{1,0:T(8,128)(2,1)} %copy-done.3, bf16[1024,128]{1,0:T(8,128)(2,1)} %copy-done.4, bf16[1024,128]{1,0:T(8,128)(2,1)} %copy-done.5), custom_call_target="tpu_custom_call" | custom-call | tf_op jit(solution)/shard_map/unpack/pallas_call | solution.py:285
  (92 shorter events, 6.1 us)
Async XLA Ops:
  0.1 44.0 %copy-start.15 = (bf16[512,512]{1,0:T(8,128)(2,1)S(1)}, bf16[512,512]{1,0:T(8,128)(2,1)}, u32[]{:S(2)}) copy-start(bf16[512,512]{1,0:T(8,128)(2,1)} %refs_8_.1) | copy-start | bytes 1572868
  10.7 8.0 %collective-permute-start = (bf16[1024,128]{1,0:T(8,128)(2,1)}, bf16[1024,128]{1,0:T(8,128)(2,1)S(1)}, u32[]{:S(2)}, u32[]{:S(2)}) collective-permute-start(bf16[1024,128]{1,0:T(8,128)(2,1)} %get-tuple-element.24), channel_id=1, source_target_pairs={{0,4},{4,8},{8,12},{12,0},{1,5},{5,9},{9,13},{13,1},{2,6},{6,10},{... | collective-permute-start | bytes 786440 | tf_op jit(solution)/shard_map/ppermute | solution.py:491
  12.9 22.2 %collective-permute-start.1 = (bf16[1024,128]{1,0:T(8,128)(2,1)}, bf16[1024,128]{1,0:T(8,128)(2,1)S(1)}, u32[]{:S(2)}, u32[]{:S(2)}) collective-permute-start(bf16[1024,128]{1,0:T(8,128)(2,1)} %get-tuple-element.25), channel_id=1, source_target_pairs={{0,8},{4,12},{8,0},{12,4},{1,9},{5,13},{9,1},{13,5},{2,10},{6,14},... | collective-permute-start | bytes 786440 | tf_op jit(solution)/shard_map/ppermute | solution.py:491
  12.9 23.2 %collective-permute-start.2 = (bf16[1024,128]{1,0:T(8,128)(2,1)}, bf16[1024,128]{1,0:T(8,128)(2,1)S(1)}, u32[]{:S(2)}, u32[]{:S(2)}) collective-permute-start(bf16[1024,128]{1,0:T(8,128)(2,1)} %get-tuple-element.26), channel_id=1, source_target_pairs={{0,12},{4,0},{8,4},{12,8},{1,13},{5,1},{9,5},{13,9},{2,14},{6,2},{... | collective-permute-start | bytes 786440 | tf_op jit(solution)/shard_map/ppermute | solution.py:491
  14.2 101.0 %copy-start.10 = (f32[1,768]{1,0:T(1,128)}, f32[1,768]{1,0:T(1,128)S(1)}, u32[]{:S(2)}) copy-start(f32[1,768]{1,0:T(1,128)S(1)} %broadcast_in_dim.28.refs_12_) | copy-start | bytes 9220
  14.2 2.1 %collective-permute-start.18 = (f32[1,768]{1,0:T(1,128)S(1)}, f32[1,768]{1,0:T(1,128)S(1)}, u32[]{:S(2)}, u32[]{:S(2)}) collective-permute-start(f32[1,768]{1,0:T(1,128)S(1)} %broadcast_in_dim.28.refs_12_), channel_id=1, source_target_pairs={{0,1},{1,0},{2,3},{3,2},{4,5},{5,4},{6,7},{7,6},{8,9},{9,8},{10,11... | collective-permute-start | bytes 9224 | tf_op jit(solution)/shard_map/ppermute | solution.py:512
  15.5 2.7 %collective-permute-start.19 = (f32[1,768]{1,0:T(1,128)S(1)}, f32[1,768]{1,0:T(1,128)S(1)}, u32[]{:S(2)}, u32[]{:S(2)}) collective-permute-start(f32[1,768]{1,0:T(1,128)S(1)} %broadcast_in_dim.28.refs_12_), channel_id=1, source_target_pairs={{0,2},{1,3},{2,0},{3,1},{4,6},{5,7},{6,4},{7,5},{8,10},{9,11},{10,... | collective-permute-start | bytes 9224 | tf_op jit(solution)/shard_map/ppermute | solution.py:509
  16.4 98.9 %copy-start.25 = (f32[1,768]{1,0:T(1,128)}, f32[1,768]{1,0:T(1,128)S(1)}, u32[]{:S(2)}) copy-start(f32[1,768]{1,0:T(1,128)S(1)} %collective-permute-done.18.refs_13_) | copy-start | bytes 9220
  16.4 30.0 %collective-permute-start.6 = (bf16[3,512,128]{2,1,0:T(8,128)(2,1)S(1)}, bf16[3,512,128]{2,1,0:T(8,128)(2,1)S(1)}, u32[]{:S(2)}, u32[]{:S(2)}) collective-permute-start(bf16[3,512,128]{2,1,0:T(8,128)(2,1)S(1)} %copy-done.20), channel_id=1, source_target_pairs={{0,1},{1,0},{2,3},{3,2},{4,5},{5,4},{6,7},{7,6},{8,9},{9,8},{10,11... | collective-permute-start | bytes 1179656 | tf_op jit(solution)/shard_map/ppermute | solution.py:512
  18.3 96.9 %copy-start.26 = (f32[1,768]{1,0:T(1,128)}, f32[1,768]{1,0:T(1,128)S(1)}, u32[]{:S(2)}) copy-start(f32[1,768]{1,0:T(1,128)S(1)} %collective-permute-done.19.refs_14_) | copy-start | bytes 9220
  18.3 27.2 %collective-permute-start.7 = (bf16[3,512,128]{2,1,0:T(8,128)(2,1)S(1)}, bf16[3,512,128]{2,1,0:T(8,128)(2,1)}, u32[]{:S(2)}, u32[]{:S(2)}) collective-permute-start(bf16[3,512,128]{2,1,0:T(8,128)(2,1)S(1)} %copy-done.20), channel_id=1, source_target_pairs={{0,2},{1,3},{2,0},{3,1},{4,6},{5,7},{6,4},{7,5},{8,10},{9,11},{10,... | collective-permute-start | bytes 1179656 | tf_op jit(solution)/shard_map/ppermute | solution.py:509
  18.7 25.3 %collective-permute-start.9 = (bf16[512,128]{1,0:T(8,128)(2,1)S(1)}, bf16[512,128]{1,0:T(8,128)(2,1)}, u32[]{:S(2)}, u32[]{:S(2)}) collective-permute-start(bf16[512,128]{1,0:T(8,128)(2,1)S(1)} %copy-done.23), channel_id=1, source_target_pairs={{0,1},{1,0},{2,3},{3,2},{4,5},{5,4},{6,7},{7,6},{8,9},{9,8},{10,11... | collective-permute-start | bytes 393224 | tf_op jit(solution)/shard_map/ppermute | solution.py:512
  35.1 9.2 %collective-permute-start.10 = (bf16[512,128]{1,0:T(8,128)(2,1)S(1)}, bf16[512,128]{1,0:T(8,128)(2,1)S(1)}, u32[]{:S(2)}, u32[]{:S(2)}) collective-permute-start(bf16[512,128]{1,0:T(8,128)(2,1)S(1)} %copy-done.23), channel_id=1, source_target_pairs={{0,2},{1,3},{2,0},{3,1},{4,6},{5,7},{6,4},{7,5},{8,10},{9,11},{10,... | collective-permute-start | bytes 393224 | tf_op jit(solution)/shard_map/ppermute | solution.py:509
  36.1 6.6 %collective-permute-start.20 = (f32[1,768]{1,0:T(1,128)S(1)}, f32[1,768]{1,0:T(1,128)S(1)}, u32[]{:S(2)}, u32[]{:S(2)}) collective-permute-start(f32[1,768]{1,0:T(1,128)S(1)} %collective-permute-done.19.refs_14_), channel_id=1, source_target_pairs={{0,1},{1,0},{2,3},{3,2},{4,5},{5,4},{6,7},{7,6},{8,9},{9,8},{10,11... | collective-permute-start | bytes 9224 | tf_op jit(solution)/shard_map/ppermute | solution.py:512
  42.7 72.5 %copy-start.27 = (f32[1,768]{1,0:T(1,128)}, f32[1,768]{1,0:T(1,128)S(1)}, u32[]{:S(2)}) copy-start(f32[1,768]{1,0:T(1,128)S(1)} %collective-permute-done.20.refs_15_) | copy-start | bytes 9220
  42.7 31.9 %collective-permute-start.13 = (bf16[512,512]{1,0:T(8,128)(2,1)S(1)}, bf16[512,512]{1,0:T(8,128)(2,1)S(1)}, u32[]{:S(2)}, u32[]{:S(2)}) collective-permute-start(bf16[512,512]{1,0:T(8,128)(2,1)S(1)} %copy-done.14), channel_id=1, source_target_pairs={{0,2},{1,3},{2,0},{3,1},{4,6},{5,7},{6,4},{7,5},{8,10},{9,11},{10,... | collective-permute-start | bytes 1572872 | tf_op jit(solution)/shard_map/ppermute | solution.py:509
  44.0 31.2 %collective-permute-start.16 = (bf16[512,512]{1,0:T(8,128)(2,1)S(1)}, bf16[512,512]{1,0:T(8,128)(2,1)S(1)}, u32[]{:S(2)}, u32[]{:S(2)}) collective-permute-start(bf16[512,512]{1,0:T(8,128)(2,1)S(1)} %copy-done.15), channel_id=1, source_target_pairs={{0,2},{1,3},{2,0},{3,1},{4,6},{5,7},{6,4},{7,5},{8,10},{9,11},{10,... | collective-permute-start | bytes 1572872 | tf_op jit(solution)/shard_map/ppermute | solution.py:509
  44.3 28.8 %collective-permute-start.4 = (bf16[1024,128]{1,0:T(8,128)(2,1)}, bf16[1024,128]{1,0:T(8,128)(2,1)S(1)}, u32[]{:S(2)}, u32[]{:S(2)}) collective-permute-start(bf16[1024,128]{1,0:T(8,128)(2,1)} %get-tuple-element.28), channel_id=1, source_target_pairs={{0,2},{1,3},{2,0},{3,1},{4,6},{5,7},{6,4},{7,5},{8,10},{9,11},{10,... | collective-permute-start | bytes 786440 | tf_op jit(solution)/shard_map/ppermute | solution.py:587
  45.5 30.2 %collective-permute-start.8 = (bf16[3,512,128]{2,1,0:T(8,128)(2,1)}, bf16[3,512,128]{2,1,0:T(8,128)(2,1)}, u32[]{:S(2)}, u32[]{:S(2)}) collective-permute-start(bf16[3,512,128]{2,1,0:T(8,128)(2,1)} %collective-permute-done.7.refs_6_), channel_id=1, source_target_pairs={{0,1},{1,0},{2,3},{3,2},{4,5},{5,4},{6,7},{7,6},{8,9},{9,8},{10,11... | collective-permute-start | bytes 1179656 | tf_op jit(solution)/shard_map/ppermute | solution.py:512
  46.4 28.3 %collective-permute-start.3 = (bf16[1024,128]{1,0:T(8,128)(2,1)}, bf16[1024,128]{1,0:T(8,128)(2,1)}, u32[]{:S(2)}, u32[]{:S(2)}) collective-permute-start(bf16[1024,128]{1,0:T(8,128)(2,1)} %get-tuple-element.27.refs_0_), channel_id=1, source_target_pairs={{0,1},{1,0},{2,3},{3,2},{4,5},{5,4},{6,7},{7,6},{8,9},{9,8},{10,11... | collective-permute-start | bytes 786440 | tf_op jit(solution)/shard_map/ppermute | solution.py:590
  73.1 2.2 %collective-permute-start.5 = (bf16[1024,128]{1,0:T(8,128)(2,1)S(1)}, bf16[1024,128]{1,0:T(8,128)(2,1)}, u32[]{:S(2)}, u32[]{:S(2)}) collective-permute-start(bf16[1024,128]{1,0:T(8,128)(2,1)S(1)} %collective-permute-done.4.refs_2_), channel_id=1, source_target_pairs={{0,1},{1,0},{2,3},{3,2},{4,5},{5,4},{6,7},{7,6},{8,9},{9,8},{10,11... | collective-permute-start | bytes 786440 | tf_op jit(solution)/shard_map/ppermute | solution.py:590
  74.6 40.7 %collective-permute-start.12 = (bf16[512,512]{1,0:T(8,128)(2,1)S(1)}, bf16[512,512]{1,0:T(8,128)(2,1)S(1)}, u32[]{:S(2)}, u32[]{:S(2)}) collective-permute-start(bf16[512,512]{1,0:T(8,128)(2,1)S(1)} %copy-done.14), channel_id=1, source_target_pairs={{0,1},{1,0},{2,3},{3,2},{4,5},{5,4},{6,7},{7,6},{8,9},{9,8},{10,11... | collective-permute-start | bytes 1572872 | tf_op jit(solution)/shard_map/ppermute | solution.py:512
  74.7 40.6 %collective-permute-start.15 = (bf16[512,512]{1,0:T(8,128)(2,1)S(1)}, bf16[512,512]{1,0:T(8,128)(2,1)S(1)}, u32[]{:S(2)}, u32[]{:S(2)}) collective-permute-start(bf16[512,512]{1,0:T(8,128)(2,1)S(1)} %copy-done.15), channel_id=1, source_target_pairs={{0,1},{1,0},{2,3},{3,2},{4,5},{5,4},{6,7},{7,6},{8,9},{9,8},{10,11... | collective-permute-start | bytes 1572872 | tf_op jit(solution)/shard_map/ppermute | solution.py:512
  75.2 40.1 %collective-permute-start.11 = (bf16[512,128]{1,0:T(8,128)(2,1)}, bf16[512,128]{1,0:T(8,128)(2,1)}, u32[]{:S(2)}, u32[]{:S(2)}) collective-permute-start(bf16[512,128]{1,0:T(8,128)(2,1)} %copy-done.24), channel_id=1, source_target_pairs={{0,1},{1,0},{2,3},{3,2},{4,5},{5,4},{6,7},{7,6},{8,9},{9,8},{10,11... | collective-permute-start | bytes 393224 | tf_op jit(solution)/shard_map/ppermute | solution.py:512
  75.3 40.0 %collective-permute-start.14 = (bf16[512,512]{1,0:T(8,128)(2,1)S(1)}, bf16[512,512]{1,0:T(8,128)(2,1)}, u32[]{:S(2)}, u32[]{:S(2)}) collective-permute-start(bf16[512,512]{1,0:T(8,128)(2,1)S(1)} %collective-permute-done.13.refs_6_), channel_id=1, source_target_pairs={{0,1},{1,0},{2,3},{3,2},{4,5},{5,4},{6,7},{7,6},{8,9},{9,8},{10,11... | collective-permute-start | bytes 1572872 | tf_op jit(solution)/shard_map/ppermute | solution.py:512
  75.7 39.6 %collective-permute-start.17 = (bf16[512,512]{1,0:T(8,128)(2,1)S(1)}, bf16[512,512]{1,0:T(8,128)(2,1)}, u32[]{:S(2)}, u32[]{:S(2)}) collective-permute-start(bf16[512,512]{1,0:T(8,128)(2,1)S(1)} %collective-permute-done.16.refs_10_), channel_id=1, source_target_pairs={{0,1},{1,0},{2,3},{3,2},{4,5},{5,4},{6,7},{7,6},{8,9},{9,8},{10,11... | collective-permute-start | bytes 1572872 | tf_op jit(solution)/shard_map/ppermute | solution.py:512
  125.1 4.5 %collective-permute-start.21 = (bf16[512,128]{1,0:T(8,128)(2,1)}, bf16[512,128]{1,0:T(8,128)(2,1)S(1)}, u32[]{:S(2)}, u32[]{:S(2)}) collective-permute-start(bf16[512,128]{1,0:T(8,128)(2,1)} %get-tuple-element.32), channel_id=1, source_target_pairs={{0,1},{1,2},{2,3},{3,0},{4,5},{5,6},{6,7},{7,4},{8,9},{9,10},{10,1... | collective-permute-start | bytes 393224 | tf_op jit(solution)/shard_map/ppermute | solution.py:491
  126.7 6.4 %collective-permute-start.22 = (bf16[512,128]{1,0:T(8,128)(2,1)}, bf16[512,128]{1,0:T(8,128)(2,1)S(1)}, u32[]{:S(2)}, u32[]{:S(2)}) collective-permute-start(bf16[512,128]{1,0:T(8,128)(2,1)} %get-tuple-element.33), channel_id=1, source_target_pairs={{0,2},{1,3},{2,0},{3,1},{4,6},{5,7},{6,4},{7,5},{8,10},{9,11},{10,... | collective-permute-start | bytes 393224 | tf_op jit(solution)/shard_map/ppermute | solution.py:491
  126.9 6.8 %collective-permute-start.23 = (bf16[512,128]{1,0:T(8,128)(2,1)}, bf16[512,128]{1,0:T(8,128)(2,1)S(1)}, u32[]{:S(2)}, u32[]{:S(2)}) collective-permute-start(bf16[512,128]{1,0:T(8,128)(2,1)} %get-tuple-element.34), channel_id=1, source_target_pairs={{0,3},{1,0},{2,1},{3,2},{4,7},{5,4},{6,5},{7,6},{8,11},{9,8},{10,9... | collective-permute-start | bytes 393224 | tf_op jit(solution)/shard_map/ppermute | solution.py:491
  139.1 8.3 %collective-permute-start.24 = (bf16[1024,128]{1,0:T(8,128)(2,1)}, bf16[1024,128]{1,0:T(8,128)(2,1)S(1)}, u32[]{:S(2)}, u32[]{:S(2)}) collective-permute-start(bf16[1024,128]{1,0:T(8,128)(2,1)} %get-tuple-element.36), channel_id=1, source_target_pairs={{0,4},{4,8},{8,12},{12,0},{1,5},{5,9},{9,13},{13,1},{2,6},{6,10},{... | collective-permute-start | bytes 786440 | tf_op jit(solution)/shard_map/ppermute | solution.py:491
  139.2 23.3 %collective-permute-start.25 = (bf16[1024,128]{1,0:T(8,128)(2,1)}, bf16[1024,128]{1,0:T(8,128)(2,1)S(1)}, u32[]{:S(2)}, u32[]{:S(2)}) collective-permute-start(bf16[1024,128]{1,0:T(8,128)(2,1)} %get-tuple-element.37), channel_id=1, source_target_pairs={{0,8},{4,12},{8,0},{12,4},{1,9},{5,13},{9,1},{13,5},{2,10},{6,14},... | collective-permute-start | bytes 786440 | tf_op jit(solution)/shard_map/ppermute | solution.py:491
  142.2 23.9 %collective-permute-start.26 = (bf16[1024,128]{1,0:T(8,128)(2,1)}, bf16[1024,128]{1,0:T(8,128)(2,1)S(1)}, u32[]{:S(2)}, u32[]{:S(2)}) collective-permute-start(bf16[1024,128]{1,0:T(8,128)(2,1)} %get-tuple-element.38), channel_id=1, source_target_pairs={{0,12},{4,0},{8,4},{12,8},{1,13},{5,1},{9,5},{13,9},{2,14},{6,2},{... | collective-permute-start | bytes 786440 | tf_op jit(solution)/shard_map/ppermute | solution.py:491
  (23 other events, 351.8 us)
